TPU v7x, 256 devices: a whole 4x4x8 slice. The times are simulated.
256 devices in a mesh: rows: 32 (over x, z), vecs: 8 (over y, core).
Axes of the slice: x: 4, y: 4, z: 8, core: 2. Of those that a mesh axis runs over, the one named last changes fastest.
Arguments:
- coords: float32 [3, 8192], P(None, ('rows', 'vecs')), may hold values from 0 to 1
- old_vectors: bfloat16 [8192, 16384], P('rows', 'vecs'), may hold values from -0.078125 to 0.078125
- pivots: int32 [2, 128], replicated, may hold values from 0 to 8191, as said below
- slots: int32 [8192], replicated, may hold values from 0 to 8191, each once
Outputs:
- new_vectors: float32 [8192, 256], P(('rows', 'vecs'))
Inputs may be any that keep to these rules, and one draw needn't show every extreme that they name: `pivots`: all 256 pivot numbers are distinct. `slots`: each window row belongs to exactly one point.
All inputs are finite; a program needn't handle non-finite values.
Results may differ from a plain program's by a relative error of at most 0.0003.
Values may be sent and summed in bfloat16 or wider, within the bound.
A program may use at most 64 MiB of HBM per device.

v0:
```python
import jax
import jax.numpy as jnp
from jax import lax
from jax.sharding import PartitionSpec as P

length_scale = 0.5
noise_shift = 12.0


def matern(points, centers):
    dist_sq = jnp.zeros((points.shape[1], centers.shape[1]), jnp.float32)
    for component in range(3):
        differ = points[component][:, None] - centers[component][None, :]
        dist_sq = dist_sq + differ * differ
    scaled = jnp.sqrt(5.0 * dist_sq) / length_scale
    return (1.0 + scaled + scaled * scaled / 3.0) * jnp.exp(-scaled)


def pick_rows(block_data, wanted, first_row):
    length = block_data.shape[0]
    offset = wanted - first_row
    inside = (offset >= 0) & (offset < length)
    bounded = jnp.clip(offset, 0, length - 1)
    fetched = jnp.take(block_data, bounded, axis=0)
    return jnp.where(inside[:, None], fetched, jnp.zeros((), block_data.dtype))


def shards(coords, old_vectors, pivots, slots):
    row_block = old_vectors.shape[0]
    share = coords.shape[1]
    panels = pivots.shape[0]
    width = pivots.shape[1]
    block_first = lax.axis_index("rows") * row_block
    share_first = block_first + lax.axis_index("vecs") * share
    wanted = jnp.take(slots, pivots.reshape(-1), axis=0)
    my_rows = share_first + jnp.arange(share, dtype=jnp.int32)
    every_point = lax.all_gather(coords, ("rows", "vecs"), axis=1, tiled=True)
    centers = jnp.take(every_point, wanted, axis=1)
    new_panels = []
    for panel in range(panels):
        chosen = wanted[panel * width : (panel + 1) * width]
        old_pivot = (
            lax.psum(pick_rows(old_vectors, chosen, block_first), "rows")
            .astype(jnp.float32)
            .astype(jnp.bfloat16)
        )

        def residual_term(first_row, length, old_pivot=old_pivot):
            return jnp.dot(old_vectors, old_pivot.T, preferred_element_type=jnp.float32)

        summed = lax.psum_scatter(
            residual_term(jnp.int32(0), share * lax.axis_size("vecs")),
            "vecs",
            scatter_dimension=0,
            tiled=True,
        )
        kernel = matern(coords, centers[:, panel * width : (panel + 1) * width])
        kernel = kernel + noise_shift * (my_rows[:, None] == chosen[None, :]).astype(jnp.float32)
        current = kernel - summed
        if panel > 0:
            stacked = new_panels[0]
            earlier = lax.psum(pick_rows(stacked, chosen, share_first), ("rows", "vecs"))
            current = current - jnp.dot(
                stacked,
                earlier.T,
                precision=lax.Precision.HIGHEST,
                preferred_element_type=jnp.float32,
            )
        block = lax.psum(pick_rows(current, chosen, share_first), ("rows", "vecs"))
        factor = jnp.linalg.cholesky(block)
        fresh = jax.scipy.linalg.solve_triangular(factor, current.T, lower=True).T
        new_panels.append(fresh)
    return jnp.concatenate(new_panels, axis=1)


def solution(mesh):
    in_specs = (P(None, ("rows", "vecs")), P("rows", "vecs"), P(), P())
    out_specs = P(("rows", "vecs"), None)
    return jax.shard_map(shards, mesh=mesh, in_specs=in_specs, out_specs=out_specs, check_vma=False)
```

profile of v0, /device:TPU:1, one launch (start us, length us, event | category | flops | bytes accessed | tf_op | source)
XLA Modules:
  0.0 1000.4 jit_solution(14306244718149790146)
XLA Ops:
  6.5 0.0 copy-start
  6.5 0.0 all-reduce.12.cloned.1.call-start
  6.5 0.8 compare_select_fusion.1
  7.3 2.0 gather_fusion
  9.3 0.7 compare_and_fusion.7
  10.1 0.0 copy-done
  10.1 0.9 gather_fusion.4
  11.0 0.0 copy-start.2
  11.0 0.9 gather_fusion.2
  12.0 0.0 copy-start.1
  12.0 1.2 select_select_fusion
  13.2 0.0 all-reduce.12.cloned.1.call-update
  13.2 0.0 reduce-scatter.7.cloned.1.call-start
  13.2 0.0 copy-done.2
  13.2 73.2 %all-gather = f32[256,32,3]{1,2,0:T(4,128)S(1)} all-gather(f32[1,32,3]{1,2,0:T(4,128)S(1)} %bitcast.66), channel_id=1, replica_groups=mesh['rows'=32,'vecs'=8] {'rows','vecs'}, dimensions={0}, use_global_device_ids=true | all-gather | bytes 98688 | tf_op jit(solution)/shard_map/all_gather | solution.py:37
  86.5 3.0 copy.23
  89.5 2.9 gather_fusion.1
  92.4 0.1 select_bitcast_fusion
  92.5 0.3 slice_reduce_fusion.2
  92.8 70.1 %all-reduce.12.cloned.1.call-done = (bf16[128,2048]{1,0:T(8,128)(2,1)}, bf16[128,2048]{1,0:T(8,128)(2,1)}) async-done(((bf16[128,2048]{1,0:T(8,128)(2,1)}, bf16[128,2048]{1,0:T(8,128)(2,1)}), (bf16[128,2048]{1,0:T(8,128)(2,1)}, bf16[128,2048]{1,0:T(8,128)(2,1)})) %all-reduce.12.cloned.1.call-update) | async-done | bytes 1048592 | tf_op jit(solution)/shard_map/psum | solution.py:43
  162.9 1.5 convolution_bitcast_fusion.1
  164.4 0.7 copy.31
  165.2 0.0 reduce-scatter.7.cloned.1.call-update
  165.2 0.0 all-reduce.6.cloned.1.call-start
  165.3 33.3 %reduce-scatter.7.cloned.1.call-done = f32[32,128]{1,0:T(8,128)} async-done(((f32[256,128]{1,0:T(8,128)}), f32[32,128]{1,0:T(8,128)}) %reduce-scatter.7.cloned.1.call-update) | async-done | bytes 16400 | tf_op jit(solution)/shard_map/reduce_scatter | solution.py:51
  198.5 0.8 add_subtract_fusion
  199.3 0.6 gather_fusion.3
  200.0 0.1 copy.25
  200.1 0.6 select_select_fusion.6
  200.7 0.0 all-reduce.6.cloned.1.call-update
  200.7 0.0 reduce-scatter.9.cloned.1.call-start
  200.8 1.5 convolution_bitcast_fusion
  202.3 0.7 copy.33
  203.1 0.0 reduce-scatter.9.cloned.1.call-update
  203.1 0.0 all-reduce.8.cloned.1.call-start
  203.1 243.7 %all-reduce.6.cloned.1.call-done = f32[128,128]{0,1:T(8,128)} async-done(((f32[128,128]{0,1:T(8,128)}), f32[128,128]{0,1:T(8,128)}) %all-reduce.6.cloned.1.call-update) | async-done | bytes 65552 | tf_op jit(solution)/shard_map/psum | solution.py:69
  446.9 0.9 copy.26
  447.8 0.9 fusion.6
  448.6 11.7 %cholesky.44 = f32[128,128]{1,0:T(8,128)S(1)} custom-call(f32[128,128]{1,0:T(8,128)S(1)} %fusion.6), custom_call_target="Cholesky" | custom-call | tf_op jit(solution)/shard_map/jit(cholesky)/cholesky | solution.py:70
  460.4 0.6 compare_reduce_fusion.1
  461.0 0.7 fusion
  461.7 9.8 custom-call.6
  471.5 0.2 fusion.4
  471.7 0.7 gather_fusion.5
  472.3 0.1 copy.28
  472.4 0.6 select_select_fusion.5
  473.1 0.0 all-reduce.8.cloned.1.call-update
  473.1 0.2 all-reduce.10.cloned.1.call-start
  473.3 3.4 reduce-scatter.9.cloned.1.call-done
  476.7 248.0 %all-reduce.8.cloned.1.call-done = f32[128,128]{0,1:T(8,128)} async-done(((f32[128,128]{0,1:T(8,128)}), f32[128,128]{0,1:T(8,128)}) %all-reduce.8.cloned.1.call-update) | async-done | bytes 65552 | tf_op jit(solution)/shard_map/psum | solution.py:62
  724.8 1.0 convolution_subtract_fusion
  725.8 0.6 gather_fusion.6
  726.5 0.1 copy.29
  726.6 0.6 select_select_fusion.4
  727.2 0.0 all-reduce.10.cloned.1.call-update
  727.2 240.9 %all-reduce.10.cloned.1.call-done = f32[128,128]{0,1:T(8,128)} async-done(((f32[128,128]{0,1:T(8,128)}), f32[128,128]{0,1:T(8,128)}) %all-reduce.10.cloned.1.call-update) | async-done | bytes 65552 | tf_op jit(solution)/shard_map/psum | solution.py:69
  968.1 0.9 copy.30
  969.0 0.9 fusion.3
  969.9 11.7 %cholesky.55 = f32[128,128]{1,0:T(8,128)S(1)} custom-call(f32[128,128]{1,0:T(8,128)S(1)} %fusion.3), custom_call_target="Cholesky" | custom-call | tf_op jit(solution)/shard_map/jit(cholesky)/cholesky | solution.py:70
  981.6 0.6 compare_reduce_fusion
  982.3 0.7 fusion.1
  983.0 9.8 custom-call.7
  992.8 0.2 convolution_bitcast_fusion.2
  992.9 0.6 pad_maximum_fusion
  (14 shorter events, 0.1 us)
Async XLA Ops:
  6.5 3.5 copy-start
  6.5 156.3 %all-reduce.12.cloned.1.call-start = ((), (), s32[]{:S(2)}) async-start(), calls=%async_computation.7 | async-start | bytes 2097152 | tf_op jit(solution)/shard_map/psum | solution.py:43
  11.0 2.2 copy-start.2
  12.0 77.5 %copy-start.1 = (s32[2,128]{1,0:T(2,128)S(1)}, s32[2,128]{1,0:T(2,128)}, u32[]{:S(2)}) copy-start(s32[2,128]{1,0:T(2,128)} %param.13) | copy-start | bytes 3076
  13.2 185.3 %reduce-scatter.7.cloned.1.call-start = ((), (), s32[]{:S(2)}) async-start(), calls=%async_computation.5 | async-start | bytes 147456 | tf_op jit(solution)/shard_map/reduce_scatter | solution.py:51
  165.2 281.7 %all-reduce.6.cloned.1.call-start = ((), (), s32[]{:S(2)}) async-start(), calls=%async_computation.2 | async-start | bytes 131072 | tf_op jit(solution)/shard_map/psum | solution.py:69
  200.7 276.0 %reduce-scatter.9.cloned.1.call-start = ((), (), s32[]{:S(2)}) async-start(), calls=%async_computation.6 | async-start | bytes 147456 | tf_op jit(solution)/shard_map/reduce_scatter | solution.py:51
  203.1 521.7 %all-reduce.8.cloned.1.call-start = ((), (), s32[]{:S(2)}) async-start(), calls=%async_computation.3 | async-start | bytes 131072 | tf_op jit(solution)/shard_map/psum | solution.py:62
  473.1 495.0 %all-reduce.10.cloned.1.call-start = ((), (), s32[]{:S(2)}) async-start(), calls=%async_computation.4 | async-start | bytes 131072 | tf_op jit(solution)/shard_map/psum | solution.py:69
Sparse Core Ops, SparseCore 0:
  13.3 149.5 all-reduce.11
  165.4 33.0 reduce-scatter.6
  204.0 242.7 all-reduce.5
  449.2 27.4 reduce-scatter.8
  482.1 242.6 all-reduce.7
  730.2 237.9 all-reduce.9
where the time goes:
time: 1000 us
  waiting for transfers between devices  839 us (84%)
  blocking collectives  73.2 us (7%)
  other arithmetic  53.6 us (5%)
  local copies, waits for them, and re-layouts  15.6 us (2%)
  between operations  13.7 us (1%)
    psum x2, waiting for transfers between devices, shards(): block = lax.psum(pick_rows(current, chosen, share_first), ('rows', 'vecs'))  485 us
    psum x1, waiting for transfers between devices, shards(): lax.psum(pick_rows(stacked, chosen, share_first), ('rows', 'vecs'))  248 us
    all_gather x1, blocking collectives, shards(): every_point = lax.all_gather(coords, ('rows', 'vecs'), axis=1, tiled=True)  73.2 us
    psum x1, waiting for transfers between devices, shards(): lax.psum(pick_rows(old_vectors, chosen, block_first), 'rows')  70.1 us
    reduce_scatter x2, waiting for transfers between devices, shards(): lax.psum_scatter(residual_term(jnp.int32(0), share * lax.axis_size('vecs'...  36.7 us
    another operation x6, other arithmetic, shards(): factor = jnp.linalg.cholesky(block)  24.8 us
    another operation x4, other arithmetic, shards(): fresh = jax.scipy.linalg.solve_triangular(factor, current.T, lower=True).T  20.9 us
  transfers between devices with their start and end apart: 6, of which 6 were waited for; matrix products, arithmetic and copies ran while one was open for 3% of the time, Pallas kernels for 0%

commit v1 on v0

v1 whole, which is shorter than its diff:
```python
import functools

import jax
import jax.numpy as jnp
from jax import lax
from jax.experimental import pallas as pl
from jax.experimental.pallas import tpu as pltpu
from jax.sharding import PartitionSpec as P

length_scale = 0.5
noise_shift = 12.0
MESH = pl.DeviceIdType.MESH

X = 4
Z = 8
V = 8
PIV = 256
HIGHEST = lax.Precision.HIGHEST


def matern(points, centers):
    dist_sq = jnp.zeros((points.shape[1], centers.shape[1]), jnp.float32)
    for component in range(3):
        differ = points[component][:, None] - centers[component][None, :]
        dist_sq = dist_sq + differ * differ
    scaled = jnp.sqrt(5.0 * dist_sq) / length_scale
    return (1.0 + scaled + scaled * scaled / 3.0) * jnp.exp(-scaled)


def dot_t(a, b):
    return lax.dot_general(a, b, (((1,), (1,)), ((), ())), preferred_element_type=jnp.float32)


def exchange(
    masked, old, spots, block_out, rows_out, spots_out,
    in_x, sum_x, in_z, cols, piv, sx, sz, sv, part_c, part_a, in_c, in_a,
    x_send, x_recv, z_send, z_recv, v_send, v_recv,
):
    row = lax.axis_index("rows")
    vec = lax.axis_index("vecs")
    x = row // Z
    z = row % Z
    chunk = PIV // X
    width = old.shape[1] // Z
    share = PIV // V

    def x_peer(k):
        return lax.rem(x + k, X)

    def z_peer(k):
        return lax.rem(z + k, Z)

    def v_peer(k):
        return lax.rem(vec + k, V)

    barrier = pltpu.get_barrier_semaphore()
    for k in range(1, X):
        pl.semaphore_signal(barrier, inc=1, device_id={"rows": x_peer(k) * Z + z, "vecs": vec}, device_id_type=MESH)
    for k in range(1, Z):
        pl.semaphore_signal(barrier, inc=1, device_id={"rows": x * Z + z_peer(k), "vecs": vec}, device_id_type=MESH)
    for k in range(1, V):
        pl.semaphore_signal(barrier, inc=1, device_id={"rows": row, "vecs": v_peer(k)}, device_id_type=MESH)
    pl.semaphore_wait(barrier, X + Z + V - 3)

    def to_x(k, src, dst, stage):
        return pltpu.make_async_remote_copy(
            src_ref=src, dst_ref=dst, send_sem=x_send.at[stage, k - 1], recv_sem=x_recv.at[stage, k - 1],
            device_id={"rows": x_peer(k) * Z + z, "vecs": vec}, device_id_type=MESH)

    def to_z(k, src, dst, stage):
        return pltpu.make_async_remote_copy(
            src_ref=src, dst_ref=dst, send_sem=z_send.at[stage, k - 1], recv_sem=z_recv.at[stage, k - 1],
            device_id={"rows": x * Z + z_peer(k), "vecs": vec}, device_id_type=MESH)

    def to_v(k, src, dst, stage):
        return pltpu.make_async_remote_copy(
            src_ref=src, dst_ref=dst, send_sem=v_send.at[stage, k - 1], recv_sem=v_recv.at[stage, k - 1],
            device_id={"rows": row, "vecs": v_peer(k)}, device_id_type=MESH)

    def start(copies):
        for copy in copies:
            copy.start()

    def wait(copies):
        for copy in copies:
            copy.wait()

    copies = [to_x(k, masked.at[pl.ds(x_peer(k) * chunk, chunk), :], in_x.at[k - 1], 0) for k in range(1, X)]
    copies += [to_x(k, spots, sx.at[k - 1], 1) for k in range(1, X)]
    start(copies)
    wait(copies)
    sum_x[...] = masked[pl.ds(x * chunk, chunk), :] + in_x[0] + in_x[1] + in_x[2]
    spots_x = spots[...] + sx[0] + sx[1] + sx[2]
    sx[0] = spots_x

    def columns(at):
        return pl.ds(pl.multiple_of(at * width, width), width)

    copies = [to_z(k, sum_x.at[:, columns(z_peer(k))], in_z.at[k - 1], 0) for k in range(1, Z)]
    copies += [to_z(k, sx.at[0], sz.at[k - 1], 1) for k in range(1, Z)]
    start(copies)
    wait(copies)
    total = sum_x[:, columns(z)]
    spots_z = sx[0]
    for k in range(Z - 1):
        total = total + in_z[k]
        spots_z = spots_z + sz[k]
    cols[:, columns(z)] = total
    sz[0] = spots_z

    copies = [to_z(k, cols.at[:, columns(z)], cols.at[:, columns(z)], 2) for k in range(1, Z)]
    start(copies)
    wait(copies)
    mine = pl.ds(x * chunk, chunk)
    piv[mine, :] = cols[...]
    copies = [to_x(k, cols, piv.at[mine, :], 2) for k in range(1, X)]
    start(copies)
    wait(copies)

    pivots = piv[...]
    part_a[...] = dot_t(pivots, pivots)
    part_c[...] = dot_t(old[...], pivots)

    def rows(at):
        return pl.ds(at * share, share)

    copies_a = [to_v(k, part_a.at[rows(v_peer(k)), :], in_a.at[k - 1], 0) for k in range(1, V)]
    copies_a += [to_v(k, sz.at[0], sv.at[k - 1], 3) for k in range(1, V)]
    copies_c = [to_v(k, part_c.at[rows(v_peer(k)), :], in_c.at[k - 1], 1) for k in range(1, V)]
    start(copies_a)
    start(copies_c)
    wait(copies_a)
    total = part_a[rows(vec), :]
    spots_v = sz[0]
    for k in range(V - 1):
        total = total + in_a[k]
        spots_v = spots_v + sv[k]
    block_out[rows(vec), :] = total
    spots_out[...] = spots_v
    copies = [to_v(k, block_out.at[rows(vec), :], block_out.at[rows(vec), :], 2) for k in range(1, V)]
    start(copies)
    wait(copies_c)
    total = part_c[rows(vec), :]
    for k in range(V - 1):
        total = total + in_c[k]
    rows_out[...] = total
    wait(copies)


def shards(coords, old_vectors, pivots, slots):
    row_block, depth = old_vectors.shape
    share = coords.shape[1]
    block_first = lax.axis_index("rows") * row_block
    share_first = block_first + lax.axis_index("vecs") * share
    wanted = jnp.take(slots, pivots.reshape(-1), axis=0)
    hot = (wanted[:, None] - block_first == jnp.arange(row_block, dtype=jnp.int32)[None, :]).astype(jnp.bfloat16)
    masked = jnp.dot(hot, old_vectors, preferred_element_type=jnp.float32).astype(jnp.bfloat16)
    hot_share = (jnp.arange(share, dtype=jnp.int32)[:, None] == wanted[None, :] - share_first).astype(jnp.float32)
    spots = jnp.sum(coords[:, :, None] * hot_share[None, :, :], axis=1)
    spots = jnp.concatenate([spots, jnp.zeros((5, PIV), jnp.float32)], axis=0)

    vmem = pl.BlockSpec(memory_space=pltpu.VMEM)
    f32 = jnp.float32
    bf16 = jnp.bfloat16
    block, rows, spots = pl.pallas_call(
        exchange,
        out_shape=(
            jax.ShapeDtypeStruct((PIV, PIV), f32),
            jax.ShapeDtypeStruct((share, PIV), f32),
            jax.ShapeDtypeStruct((8, PIV), f32),
        ),
        in_specs=[vmem] * 3,
        out_specs=(vmem,) * 3,
        scratch_shapes=[
            pltpu.VMEM((X - 1, PIV // X, depth), bf16),
            pltpu.VMEM((PIV // X, depth), bf16),
            pltpu.VMEM((Z - 1, PIV // X, depth // Z), bf16),
            pltpu.VMEM((PIV // X, depth), bf16),
            pltpu.VMEM((PIV, depth), bf16),
            pltpu.VMEM((X - 1, 8, PIV), f32),
            pltpu.VMEM((Z - 1, 8, PIV), f32),
            pltpu.VMEM((V - 1, 8, PIV), f32),
            pltpu.VMEM((row_block, PIV), f32),
            pltpu.VMEM((PIV, PIV), f32),
            pltpu.VMEM((V - 1, share, PIV), f32),
            pltpu.VMEM((V - 1, PIV // V, PIV), f32),
            pltpu.SemaphoreType.DMA((3, X - 1)),
            pltpu.SemaphoreType.DMA((3, X - 1)),
            pltpu.SemaphoreType.DMA((3, Z - 1)),
            pltpu.SemaphoreType.DMA((3, Z - 1)),
            pltpu.SemaphoreType.DMA((4, V - 1)),
            pltpu.SemaphoreType.DMA((4, V - 1)),
        ],
        compiler_params=pltpu.CompilerParams(collective_id=0, has_side_effects=True),
    )(masked, old_vectors, spots)

    centers = spots[:3]
    my_rows = share_first + jnp.arange(share, dtype=jnp.int32)
    diagonal = noise_shift * jnp.eye(PIV, dtype=f32)
    block = matern(centers, centers) + diagonal - block
    current = matern(coords, centers) + noise_shift * (my_rows[:, None] == wanted[None, :]).astype(f32) - rows
    factor = jnp.linalg.cholesky(block, symmetrize_input=False)
    return jax.scipy.linalg.solve_triangular(factor, current.T, lower=True).T


def solution(mesh):
    in_specs = (P(None, ("rows", "vecs")), P("rows", "vecs"), P(), P())
    out_specs = P(("rows", "vecs"), None)
    return jax.shard_map(shards, mesh=mesh, in_specs=in_specs, out_specs=out_specs, check_vma=False)
```

time: 1000 us -> 136 us (0.14)
  waiting for transfers between devices: 839 us -> 0 us
  blocking collectives: 73.2 us -> 0 us
  Pallas kernels: 0 us -> 67 us
  between operations: 13.7 us -> 1.55 us
    psum x4 -> x0, waiting for transfers between devices: 803 us -> none  [the longest x2 485 us: shards(): block = lax.psum(pick_rows(current, chosen, share_first), ('rows', 'vecs'))]
    all_gather x1 -> x0, blocking collectives: 73.2 us -> none  [shards(): every_point = lax.all_gather(coords, ('rows', 'vecs'), axis=1, tiled=True)]
    pallas_call x0 -> x1, Pallas kernels: none -> 67 us  [shards(): pl.pallas_call(exchange, out_shape=(jax.ShapeDtypeStruct((PIV, PIV), f32)...]
    reduce_scatter x2 -> x0, waiting for transfers between devices: 36.7 us -> none  [shards(): lax.psum_scatter(residual_term(jnp.int32(0), share * lax.axis_size('vecs'...]
    another operation x10 -> x9, other arithmetic: 45.7 us -> 53.8 us  [the longest x6 34.1 us: shards(): factor = jnp.linalg.cholesky(block, symmetrize_input=False)]
  transfers between devices with their start and end apart: 6 -> 0, of which waited for: 6 -> 0; matrix products, arithmetic and copies ran while one was open for 3% -> 0% of each run, Pallas kernels for 0% -> 0%
where the time goes in v1:
time: 136 us
  Pallas kernels  67 us (49%)
  other arithmetic  57.5 us (42%)
  local copies, waits for them, and re-layouts  7.28 us (5%)
  matrix products  2.47 us (2%)
  between operations  1.55 us (1%)
    pallas_call x1, Pallas kernels, shards(): pl.pallas_call(exchange, out_shape=(jax.ShapeDtypeStruct((PIV, PIV), f32)...  67 us
    another operation x6, other arithmetic, shards(): factor = jnp.linalg.cholesky(block, symmetrize_input=False)  34.1 us
    another operation x3, other arithmetic, shards(): return jax.scipy.linalg.solve_triangular(factor, current.T, lower=True).T  19.7 us
    another operation x6, local copies, waits for them, and re-layouts  4.02 us

profile of v1, /device:TPU:1, one launch (start us, length us, event | category | flops | bytes accessed | tf_op | source)
XLA Modules:
  0.0 135.8 jit_solution(13174487319322664466)
XLA Ops:
  0.0 0.0 copy-start
  0.0 0.0 copy-start.3
  0.0 0.0 copy-start.1
  0.0 0.8 compare_select_fusion
  0.8 0.0 copy-done
  0.8 1.7 %gather_fusion = s32[256]{0:T(256)S(1)} fusion(s32[8192]{0:T(1024)S(1)} %copy-done, s32[1024]{0:T(1024)S(1)} %pad_clamp_fusion), kind=kCustom, calls=%fused_computation | custom fusion | bytes 3072 | tf_op jit(solution)/shard_map/jit(_take)/gather | solution.py:155
  2.5 0.0 copy-done.3
  2.6 0.0 copy-done.1
  2.6 0.0 copy-start.2
  2.6 1.5 %convolution_convert_fusion.masked = bf16[256,2048]{1,0:T(8,128)(2,1)} fusion(bf16[256,2048]{1,0:T(8,128)(2,1)S(1)} %copy-done.1, s32[256]{0:T(256)S(1)} %broadcast_subtract_fusion.1), kind=kOutput, calls=%fused_computation.3 | convolution fusion | flops 269025280 | bytes 2098176 | tf_op jit(solution)/shard_map/dot_general | solution.py:157
  4.1 0.0 copy-done.2
  4.1 0.1 multiply_reduce_fusion
  4.2 0.6 concatenate.6.spots
  4.8 67.0 %shard_map.46 = (f32[256,256]{1,0:T(8,128)}, f32[32,256]{1,0:T(8,128)}, f32[8,256]{1,0:T(8,128)}) custom-call(bf16[256,2048]{1,0:T(8,128)(2,1)} %convolution_convert_fusion.masked, bf16[256,2048]{1,0:T(8,128)(2,1)} %old.1, f32[8,256]{1,0:T(8,128)} %concatenate.6.spots), custom_call_target="tpu_custom_call" | custom-call | tf_op jit(solution)/shard_map/pallas_call | solution.py:165
  71.8 0.8 fusion.10
  72.6 0.9 subtract_bitcast_fusion
  73.5 1.3 add_subtract_fusion
  74.7 11.7 %cholesky.49 = f32[128,128]{1,0:T(8,128)S(1)} custom-call(f32[128,128]{1,0:T(8,128)S(1)} %cholesky.115), custom_call_target="Cholesky" | custom-call | tf_op jit(solution)/shard_map/jit(cholesky)/cholesky | solution.py:202
  86.5 9.8 %custom-call.15 = f32[1,128,128]{1,2,0:T(8,128)S(1)} custom-call(f32[1,128,128]{2,1,0:T(8,128)S(1)} %get-tuple-element.34), custom_call_target="InvertDiagBlocksLowerTriangular" | custom-call | tf_op jit(solution)/shard_map/jit(cholesky)/cholesky | solution.py:202
  96.3 0.2 constant_dynamic-update-slice_fusion.1
  96.6 0.3 convolution_subtract_fusion
  96.8 11.8 %cholesky.103 = f32[128,128]{1,0:T(8,128)S(1)} custom-call(f32[128,128]{1,0:T(8,128)S(1)} %convolution_subtract_fusion), custom_call_target="Cholesky" | custom-call | tf_op jit(solution)/shard_map/jit(cholesky)/cholesky | solution.py:202
  108.7 0.7 compare_reduce_fusion
  110.8 0.1 triangular_solve.66
  110.9 4.1 %while.1 = (s32[]{:T(128)}, f32[256,256]{1,0:T(8,128)S(1)}, s32[2,2]{1,0:T(2,128)S(1)}, f32[2,128,128]{2,1,0:T(8,128)S(1)}, s32[]{:T(128)}) while((s32[]{:T(128)}, f32[256,256]{1,0:T(8,128)S(1)}, s32[2,2]{1,0:T(2,128)S(1)}, f32[2,128,128]{2,1,0:T(8,128)S(1)}, s32[]{:T(128)}) %tuple.28), condition=%wide.while_cond, body=%wide.while_body.sunk | while | flops 2 | bytes 131181 | solution.py:203
  110.9 0.7 fusion.17
  111.5 1.3 bitcast_dynamic-update-slice_fusion.2
  112.9 0.7 fusion.17
  113.6 1.3 bitcast_dynamic-update-slice_fusion.2
  114.9 19.7 %custom-call.16 = f32[2,128,128]{1,2,0:T(8,128)S(1)} custom-call(f32[2,128,128]{2,1,0:T(8,128)S(1)} %get-tuple-element.18), custom_call_target="InvertDiagBlocksLowerTriangular" | custom-call | tf_op jit(solution)/shard_map/jit(_solve_triangular)/triangular_solve | solution.py:203
  134.6 0.2 fusion.3
  134.8 0.2 convolution_subtract_fusion.1
  135.0 0.2 fusion.2
  135.2 0.6 maximum_bitcast_fusion
  (15 shorter events, 0.2 us)
Async XLA Ops:
  0.0 0.8 copy-start
  0.0 2.5 %copy-start.3 = (s32[2,128]{1,0:T(2,128)S(1)}, s32[2,128]{1,0:T(2,128)}, u32[]{:S(2)}) copy-start(s32[2,128]{1,0:T(2,128)} %param.6) | copy-start | bytes 3076
  0.0 2.6 %copy-start.1 = (bf16[256,2048]{1,0:T(8,128)(2,1)S(1)}, bf16[256,2048]{1,0:T(8,128)(2,1)}, u32[]{:S(2)}) copy-start(bf16[256,2048]{1,0:T(8,128)(2,1)} %old.1) | copy-start | bytes 3145732
  2.6 1.5 %copy-start.2 = (f32[3,32]{1,0:T(4,128)S(1)}, f32[3,32]{1,0:T(4,128)}, u32[]{:S(2)}) copy-start(f32[3,32]{1,0:T(4,128)} %param.4) | copy-start | bytes 1156

commit v2 on v1

--- a/solution.py
+++ b/solution.py
@@ -15,16 +15,114 @@
 Z = 8
 V = 8
 PIV = 256
-HIGHEST = lax.Precision.HIGHEST
-
-
-def matern(points, centers):
-    dist_sq = jnp.zeros((points.shape[1], centers.shape[1]), jnp.float32)
-    for component in range(3):
-        differ = points[component][:, None] - centers[component][None, :]
-        dist_sq = dist_sq + differ * differ
-    scaled = jnp.sqrt(5.0 * dist_sq) / length_scale
-    return (1.0 + scaled + scaled * scaled / 3.0) * jnp.exp(-scaled)
+G = 8
+LANES = 128
+
+
+def column_of(row, length):
+    eye = lax.broadcasted_iota(jnp.int32, (length, length), 0) == lax.broadcasted_iota(jnp.int32, (length, length), 1)
+    return jnp.sum(jnp.where(eye, row, 0.0), axis=1, keepdims=True)
+
+
+def kernel_value(points, centers):
+    dist_sq = None
+    for a, b in zip(points, centers):
+        differ = a - b
+        dist_sq = differ * differ if dist_sq is None else dist_sq + differ * differ
+    scaled = jnp.sqrt(5.0 * dist_sq) * 2.0
+    return (1.0 + scaled + scaled * scaled * (1.0 / 3.0)) * jnp.exp(-scaled)
+
+
+def finish(block, rows, spots, coords, place, out, mat):
+    share = rows.shape[0]
+    tiles = PIV // LANES
+    centers = [spots[c : c + 1, :] for c in range(3)]
+    for t in range(tiles):
+        lanes = slice(t * LANES, (t + 1) * LANES)
+        points = [column_of(spots[c : c + 1, lanes], LANES) for c in range(3)]
+        value = kernel_value(points, centers)
+        at = lax.broadcasted_iota(jnp.int32, (LANES, PIV), 0) + t * LANES
+        value = value + jnp.where(at == lax.broadcasted_iota(jnp.int32, (LANES, PIV), 1), 12.0, 0.0)
+        mat[lanes, :] = value - block[lanes, :]
+    points = [column_of(coords[c : c + 1, :], share) for c in range(3)]
+    value = kernel_value(points, centers)
+    at = lax.broadcasted_iota(jnp.int32, (share, PIV), 0)
+    value = value + jnp.where(at == place[...], 12.0, 0.0)
+    mat[PIV : PIV + share, :] = value - rows[...]
+
+    lane = lax.broadcasted_iota(jnp.int32, (G, LANES), 1)
+    full = (G, LANES)
+    groups_all = (PIV + share) // G
+    for k in range(PIV // G):
+        first = k * G
+        tile = first // LANES
+        off = first % LANES
+        own = slice(first, first + G)
+        home = slice(tile * LANES, (tile + 1) * LANES)
+        diag = mat[own, home]
+        col = [jnp.broadcast_to(diag[:, off + m : off + m + 1], full) for m in range(G)]
+        s = [[None] * G for _ in range(G)]
+        for m in range(G):
+            for i in range(m, G):
+                s[i][m] = jnp.broadcast_to(col[m][i : i + 1, :], full)
+        inv = [None] * G
+        for m in range(G):
+            inv[m] = lax.rsqrt(s[m][m])
+            for i in range(m + 1, G):
+                s[i][m] = s[i][m] * inv[m]
+            for n in range(m + 1, G):
+                for i in range(n, G):
+                    s[i][n] = s[i][n] - s[i][m] * s[n][m]
+        live = range(tile, tiles)
+        u = {}
+        w = {}
+        for t in live:
+            lanes = slice(t * LANES, (t + 1) * LANES)
+            part = mat[own, lanes]
+            us = []
+            for i in range(G):
+                value = jnp.broadcast_to(part[i : i + 1, :], full)
+                for m in range(i):
+                    value = value - s[i][m] * us[m]
+                us.append(value * inv[i])
+            ws = [None] * G
+            for i in reversed(range(G)):
+                value = us[i]
+                for m in range(i + 1, G):
+                    value = value - s[m][i] * ws[m]
+                ws[i] = value * inv[i]
+            u[t], w[t] = us, ws
+        for g in range(k + 1, groups_all):
+            at = slice(g * G, (g + 1) * G)
+            source = mat[at, home]
+            cols = [jnp.broadcast_to(source[:, off + m : off + m + 1], full) for m in range(G)]
+            if g < PIV // G:
+                for t in live:
+                    lanes = slice(t * LANES, (t + 1) * LANES)
+                    value = source if t == tile else mat[at, lanes]
+                    acc = cols[0] * w[t][0]
+                    for m in range(1, G):
+                        acc = acc + cols[m] * w[t][m]
+                    mat[at, lanes] = value - acc
+            else:
+                made = []
+                for i in range(G):
+                    value = cols[i]
+                    for m in range(i):
+                        value = value - s[i][m] * made[m]
+                    made.append(value * inv[i])
+                for t in live:
+                    lanes = slice(t * LANES, (t + 1) * LANES)
+                    value = source if t == tile else mat[at, lanes]
+                    acc = made[0] * u[t][0]
+                    for m in range(1, G):
+                        acc = acc + made[m] * u[t][m]
+                    value = value - acc
+                    if t == tile:
+                        for i in range(G):
+                            value = jnp.where(lane == off + i, made[i], value)
+                    mat[at, lanes] = value
+    out[...] = mat[PIV : PIV + share, :]
 
 
 def dot_t(a, b):
@@ -194,13 +292,13 @@
         compiler_params=pltpu.CompilerParams(collective_id=0, has_side_effects=True),
     )(masked, old_vectors, spots)
 
-    centers = spots[:3]
-    my_rows = share_first + jnp.arange(share, dtype=jnp.int32)
-    diagonal = noise_shift * jnp.eye(PIV, dtype=f32)
-    block = matern(centers, centers) + diagonal - block
-    current = matern(coords, centers) + noise_shift * (my_rows[:, None] == wanted[None, :]).astype(f32) - rows
-    factor = jnp.linalg.cholesky(block, symmetrize_input=False)
-    return jax.scipy.linalg.solve_triangular(factor, current.T, lower=True).T
+    return pl.pallas_call(
+        finish,
+        out_shape=jax.ShapeDtypeStruct((share, PIV), f32),
+        in_specs=[vmem] * 5,
+        out_specs=vmem,
+        scratch_shapes=[pltpu.VMEM((PIV + share, PIV), f32)],
+    )(block, rows, spots, coords, (wanted - share_first)[None, :])
 
 
 def solution(mesh):

time: 136 us -> 85.8 us (0.63)
  other arithmetic: 57.5 us -> 1.47 us
  Pallas kernels: 67 us -> 80.3 us
  local copies, waits for them, and re-layouts: 7.28 us -> 2.35 us
  between operations: 1.55 us -> 0.06 us
    another operation x9 -> x0, other arithmetic: 53.8 us -> none  [the longest x6 34.1 us: shards(): factor = jnp.linalg.cholesky(block, symmetrize_input=False)]
    pallas_call x0 -> x1, Pallas kernels: none -> 13.4 us  [shards(): pl.pallas_call(finish, out_shape=jax.ShapeDtypeStruct((share, PIV), f32),...]
    another operation x9 -> x0, local copies, waits for them, and re-layouts: 4.12 us -> none
    transpose x2 -> x0, other arithmetic: 1.49 us -> none  [shards(): return jax.scipy.linalg.solve_triangular(factor, current.T, lower=True).T]
where the time goes in v2:
time: 85.8 us; the launch traced here: 85.7 us
  Pallas kernels  80.3 us (94%)
  local copies, waits for them, and re-layouts  2.35 us (3%)
  other arithmetic  1.47 us (2%)
  matrix products  1.45 us (2%)
    pallas_call x1, Pallas kernels, shards(): pl.pallas_call(exchange, out_shape=(jax.ShapeDtypeStruct((PIV, PIV), f32)...  66.9 us
    pallas_call x1, Pallas kernels, shards(): pl.pallas_call(finish, out_shape=jax.ShapeDtypeStruct((share, PIV), f32),...  13.4 us
    gather x1, local copies, waits for them, and re-layouts, shards(): wanted = jnp.take(slots, pivots.reshape(-1), axis=0)  1.72 us

profile of v2, /device:TPU:1, one launch (start us, length us, event | category | flops | bytes accessed | tf_op | source)
XLA Modules:
  0.0 85.7 jit_solution(14198464484031181110)
XLA Ops:
  0.0 0.0 copy-start
  0.0 0.0 copy-start.2
  0.0 0.0 copy-start.1
  0.0 0.0 copy-start.3
  0.0 0.8 compare_select_fusion.1
  0.8 0.0 copy-done
  0.8 1.7 %gather_fusion = s32[256]{0:T(256)S(1)} fusion(s32[8192]{0:T(1024)S(1)} %copy-done, s32[1024]{0:T(1024)S(1)} %pad_clamp_fusion), kind=kCustom, calls=%fused_computation | custom fusion | bytes 3072 | tf_op jit(solution)/shard_map/jit(_take)/gather | solution.py:253
  2.5 0.0 copy-done.2
  2.6 0.6 fusion.2.place
  3.2 0.0 copy-done.3
  3.2 0.1 multiply_reduce_fusion
  3.3 0.6 concatenate.3.spots
  3.9 0.0 copy-done.1
  3.9 1.5 %convolution_convert_fusion.masked = bf16[256,2048]{1,0:T(8,128)(2,1)} fusion(bf16[256,2048]{1,0:T(8,128)(2,1)S(1)} %copy-done.1, s32[256]{0:T(256)S(1)} %get-tuple-element.12), kind=kOutput, calls=%fused_computation.1 | convolution fusion | flops 269025280 | bytes 2098176 | tf_op jit(solution)/shard_map/dot_general | solution.py:255
  5.3 66.9 %shard_map.46 = (f32[256,256]{1,0:T(8,128)}, f32[32,256]{1,0:T(8,128)}, f32[8,256]{1,0:T(8,128)}) custom-call(bf16[256,2048]{1,0:T(8,128)(2,1)} %convolution_convert_fusion.masked, bf16[256,2048]{1,0:T(8,128)(2,1)} %old.1, f32[8,256]{1,0:T(8,128)} %concatenate.3.spots), custom_call_target="tpu_custom_call" | custom-call | tf_op jit(solution)/shard_map/pallas_call | solution.py:263
  72.3 13.4 %shard_map.47 = f32[32,256]{1,0:T(8,128)} custom-call(f32[256,256]{1,0:T(8,128)} %get-tuple-element.8.block, f32[32,256]{1,0:T(8,128)} %get-tuple-element.9.rows, f32[8,256]{1,0:T(8,128)} %get-tuple-element.10.spots, f32[3,32]{1,0:T(4,128)} %coords.1, s32[1,256]{1,0:T(1,128)} %fusion.2.place), custom_call_target="tpu_custom_call" | custom-call | tf_op jit(solution)/shard_map/pallas_call | solution.py:295
  (3 shorter events, 0.0 us)
Async XLA Ops:
  0.0 0.8 copy-start
  0.0 2.5 %copy-start.2 = (s32[2,128]{1,0:T(2,128)S(1)}, s32[2,128]{1,0:T(2,128)}, u32[]{:S(2)}) copy-start(s32[2,128]{1,0:T(2,128)} %param.6) | copy-start | bytes 3076
  0.0 3.9 %copy-start.1 = (bf16[256,2048]{1,0:T(8,128)(2,1)S(1)}, bf16[256,2048]{1,0:T(8,128)(2,1)}, u32[]{:S(2)}) copy-start(bf16[256,2048]{1,0:T(8,128)(2,1)} %old.1) | copy-start | bytes 3145732
  0.0 3.1 %copy-start.3 = (f32[3,32]{1,0:T(4,128)S(1)}, f32[3,32]{1,0:T(4,128)}, u32[]{:S(2)}) copy-start(f32[3,32]{1,0:T(4,128)} %coords.1) | copy-start | bytes 1156
